TPU v7x, 32 devices: a whole 2x2x4 slice. The times are simulated.
32 devices in a mesh: wide: 8 (over z, x), narrow: 4 (over y, core).
Axes of the slice: x: 2, y: 2, z: 4, core: 2. Of those that a mesh axis runs over, the one named last changes fastest.
Arguments:
- block_input: bfloat16 [12288, 768], P('wide')
- cotangent: bfloat16 [12288, 768], P('wide'), may hold values from -6 to 6
- lengths: int32 [16, 12], P('wide'), may hold values from 0 to 384, as said below
- project_weight: float32 [3, 768, 768], P(None, 'wide', 'narrow'), may hold values from -0.125 to 0.125
- output_weight: float32 [768, 768], P('narrow', 'wide'), may hold values from -1.25 to 1.25
- expand_weight: float32 [2, 768, 2048], P(None, 'wide', 'narrow'), may hold values from -0.21875 to 0.21875
- shrink_weight: float32 [2048, 768], P('narrow', 'wide'), may hold values from -0.1875 to 0.1875
- bucket_bias: float32 [32, 12], replicated, may hold values from -3 to 3
- norm_gains: float32 [2, 768], P(None, 'wide'), may hold values from 0.5 to 1.5
- project_first: float32 [3, 768, 768], P(None, 'wide', 'narrow'), may hold values from -0.00061035156 to 0.00061035156
- output_first: float32 [768, 768], P('narrow', 'wide'), may hold values from -7.6293945e-05 to 7.6293945e-05
- expand_first: float32 [2, 768, 2048], P(None, 'wide', 'narrow'), may hold values from -0.00015258789 to 0.00015258789
- shrink_first: float32 [2048, 768], P('narrow', 'wide'), may hold values from -0.00015258789 to 0.00015258789
- bucket_first: float32 [32, 12], replicated, may hold values from -0.00010681152 to 0.00010681152
- gains_first: float32 [2, 768], P(None, 'wide'), may hold values from -0.00048828125 to 0.00048828125
- project_second: float32 [3, 768, 768], P(None, 'wide', 'narrow'), may hold values from 4.3798376e-10 to 7.064254e-09
- output_second: float32 [768, 768], P('narrow', 'wide'), may hold values from 6.3578288e-12 to 1.0172526e-10
- expand_second: float32 [2, 768, 2048], P(None, 'wide', 'narrow'), may hold values from 2.5431315e-11 to 4.0972675e-10
- shrink_second: float32 [2048, 768], P('narrow', 'wide'), may hold values from 2.5431315e-11 to 4.0972675e-10
- bucket_second: float32 [32, 12], replicated, may hold values from 1.1302807e-11 to 1.8084491e-10
- gains_second: float32 [2, 768], P(None, 'wide'), may hold values from 2.8257016e-10 to 4.5211226e-09
Outputs:
- block_output: bfloat16 [12288, 768], P('wide')
- input_gradient: bfloat16 [12288, 768], P('wide')
- global_norm: float32 [], replicated
- new_project: float32 [3, 768, 768], P(None, 'wide', 'narrow')
- new_output: float32 [768, 768], P('narrow', 'wide')
- new_expand: float32 [2, 768, 2048], P(None, 'wide', 'narrow')
- new_shrink: float32 [2048, 768], P('narrow', 'wide')
- new_bucket: float32 [32, 12], replicated
- new_gains: float32 [2, 768], P(None, 'wide')
- project_first_new: float32 [3, 768, 768], P(None, 'wide', 'narrow')
- output_first_new: float32 [768, 768], P('narrow', 'wide')
- expand_first_new: float32 [2, 768, 2048], P(None, 'wide', 'narrow')
- shrink_first_new: float32 [2048, 768], P('narrow', 'wide')
- bucket_first_new: float32 [32, 12], replicated
- gains_first_new: float32 [2, 768], P(None, 'wide')
- project_second_new: float32 [3, 768, 768], P(None, 'wide', 'narrow')
- output_second_new: float32 [768, 768], P('narrow', 'wide')
- expand_second_new: float32 [2, 768, 2048], P(None, 'wide', 'narrow')
- shrink_second_new: float32 [2048, 768], P('narrow', 'wide')
- bucket_second_new: float32 [32, 12], replicated
- gains_second_new: float32 [2, 768], P(None, 'wide')
Inputs may be any that keep to these rules, and one draw needn't show every extreme that they name: Each row lists one buffer's passage lengths in packing order, each from 64 to 384, followed by zeros; a row sums to at most 768, and every row holds one passage of exactly 384 tokens.
All inputs are finite; a program needn't handle non-finite values.
Results may differ from a plain program's by a relative error of at most 0.013.
The roundings to bfloat16 on the way count: a program that leaves them out, or rounds other values in their place, can miss the bound.
Values may be sent and summed in bfloat16 or wider, within the bound.
A program may use at most 128 MiB of HBM per device.

v0:
```python
import jax
import jax.numpy as jnp
from jax import lax
from jax.sharding import PartitionSpec as P

DH = 64
STEP = 10
bucket_edges = (12, 16, 23, 32, 46, 64, 91)
norm_eps = 1e-06
clip_limit = 1.0
beta_one = 0.9
beta_two = 0.999
adam_eps = 1e-08
step_rates = (0.06, 0.3, 0.07, 0.06, 1.0, 0.3)
decay_rates = (0.01, 0.01, 0.01, 0.01, 0.0, 0.0)
masked_score = -1000000000.0


def bucket_of(offsets):
    distance = jnp.abs(offsets)
    far_bucket = 8 + sum(((distance >= threshold).astype(jnp.int32) for threshold in bucket_edges))
    return jnp.where(distance < 8, distance, far_bucket) + 16 * (offsets > 0).astype(jnp.int32)


def rms_scale(values):
    return lax.rsqrt(jnp.mean(values * values, axis=-1, keepdims=True) + norm_eps)


def norm_back(values, scale_vec, gain_vec, upstream):
    weighted = upstream * gain_vec
    inner_mean = jnp.mean(weighted * values, axis=-1, keepdims=True)
    return scale_vec * weighted - values * (scale_vec * scale_vec * scale_vec) * inner_mean


def toeplitz_rows(values, length):
    padded = jnp.concatenate([values, jnp.zeros((1,), values.dtype)])
    tiled_flat = jnp.tile(padded, length)[: length * (2 * length - 1)]
    return tiled_flat.reshape(length, 2 * length - 1)[:, length - 1 :]


def diagonal_sums(matrix, length):
    padded = jnp.pad(matrix, ((0, 0), (length - 1, 1)))
    flat_vals = jnp.concatenate([padded.reshape(-1), jnp.zeros((length,), matrix.dtype)])
    return jnp.sum(flat_vals.reshape(length, 2 * length + 1), axis=0)[: 2 * length - 1]


def adam_update(weight, moment_one, moment_two, gradient, step_rate, decay_rate):
    new_first = beta_one * moment_one + (1.0 - beta_one) * gradient
    new_second = beta_two * moment_two + (1.0 - beta_two) * gradient * gradient
    first_hat = new_first / (1.0 - beta_one**STEP)
    second_hat = new_second / (1.0 - beta_two**STEP)
    new_weight = weight - step_rate * (
        first_hat / (jnp.sqrt(second_hat) + adam_eps) + decay_rate * weight
    )
    return (new_weight, new_first, new_second)


def body(
    block_input,
    cotangent,
    lengths,
    project_weight,
    output_weight,
    expand_weight,
    shrink_weight,
    bucket_bias,
    norm_gains,
    project_first,
    output_first,
    expand_first,
    shrink_first,
    bucket_first,
    gains_first,
    project_second,
    output_second,
    expand_second,
    shrink_second,
    bucket_second,
    gains_second,
):
    tokens, model_width = block_input.shape
    buffers = lengths.shape[0]
    length = tokens // buffers
    head_width = project_weight.shape[2]
    heads_local = head_width // DH
    hidden_local = expand_weight.shape[2]
    low_gains = norm_gains.astype(jnp.bfloat16)
    project_all, output_all, expand_all, shrink_all, gains_all = (
        lax.all_gather(project_weight.astype(jnp.bfloat16), "wide", axis=1, tiled=True),
        lax.all_gather(output_weight.astype(jnp.bfloat16), "wide", axis=1, tiled=True),
        lax.all_gather(expand_weight.astype(jnp.bfloat16), "wide", axis=1, tiled=True),
        lax.all_gather(shrink_weight.astype(jnp.bfloat16), "wide", axis=1, tiled=True),
        lax.all_gather(low_gains, "wide", axis=1, tiled=True),
    )
    gain_one = gains_all[0].astype(jnp.float32)
    gain_two = gains_all[1].astype(jnp.float32)
    positions = jnp.arange(length, dtype=jnp.int32)
    segment_ends = jnp.cumsum(lengths, axis=1)
    segment_ids = jnp.sum(
        (positions[None, :, None] >= segment_ends[:, None, :]).astype(jnp.int32), axis=2
    )
    offsets = jnp.arange(2 * length - 1, dtype=jnp.int32) - (length - 1)
    onehot = (
        bucket_of(offsets)[:, None] == jnp.arange(bucket_bias.shape[0], dtype=jnp.int32)[None, :]
    ).astype(jnp.float32)
    head_start = lax.axis_index("narrow") * heads_local
    bias_local = lax.dynamic_slice_in_dim(bucket_bias, head_start, heads_local, 1)
    head_bias = jnp.dot(onehot, bias_local, precision=lax.Precision.HIGHEST).T
    input_float = block_input.astype(jnp.float32)
    scale_one = rms_scale(input_float)
    normed_one = (input_float * scale_one * gain_one).astype(jnp.bfloat16)
    project_flat = jnp.transpose(project_all, (1, 0, 2)).reshape(model_width, 3 * head_width)
    qkv_rows = jnp.dot(normed_one, project_flat, preferred_element_type=jnp.float32).astype(
        jnp.bfloat16
    )
    buffer_rows = qkv_rows.reshape(buffers, length, 3 * head_width)

    def head_scores(query_rows, key_rows, bias_row, same_segment):
        scores = jnp.einsum("qd,kd->qk", query_rows, key_rows, preferred_element_type=jnp.float32)
        scores = scores + toeplitz_rows(bias_row, length)
        return jnp.where(same_segment, scores, masked_score)

    def split_heads(block_rows):
        return block_rows.reshape(length, 3, heads_local, DH).transpose(1, 2, 0, 3)

    def buffer_forward(block_items):
        block_rows, segment_row = block_items
        pieces = split_heads(block_rows)
        same_segment = segment_row[:, None] == segment_row[None, :]

        def head_forward(head_items):
            query_rows, key_rows, value_rows, bias_row = head_items
            scores = head_scores(query_rows, key_rows, bias_row, same_segment)
            row_max = jnp.max(scores, axis=1, keepdims=True)
            log_total = row_max + jnp.log(jnp.sum(jnp.exp(scores - row_max), axis=1, keepdims=True))
            attention_probs = jnp.exp(scores - log_total).astype(jnp.bfloat16)
            head_out = jnp.dot(
                attention_probs, value_rows, preferred_element_type=jnp.float32
            ).astype(jnp.bfloat16)
            return (head_out, log_total[:, 0])

        head_outs, log_rows = lax.map(head_forward, (pieces[0], pieces[1], pieces[2], head_bias))
        return (head_outs.transpose(1, 0, 2).reshape(length, head_width), log_rows)

    attended, log_totals = lax.map(buffer_forward, (buffer_rows, segment_ids))
    attended = attended.reshape(tokens, head_width)
    attention_terms = jnp.dot(attended, output_all, preferred_element_type=jnp.float32)
    middle = input_float + lax.psum(attention_terms, "narrow")
    scale_two = rms_scale(middle)
    normed_two = (middle * scale_two * gain_two).astype(jnp.bfloat16)
    expand_flat = jnp.transpose(expand_all, (1, 0, 2)).reshape(model_width, 2 * hidden_local)
    gate_up = jnp.dot(normed_two, expand_flat, preferred_element_type=jnp.float32)
    gate_pre = gate_up[:, :hidden_local]
    up_pre = gate_up[:, hidden_local:]
    activated, gelu_pull = jax.vjp(
        lambda gate_vals: jax.nn.gelu(gate_vals, approximate=True), gate_pre
    )
    hidden = (activated * up_pre).astype(jnp.bfloat16)
    feedforward_terms = jnp.dot(hidden, shrink_all, preferred_element_type=jnp.float32)
    block_output = (
        middle + lax.psum(feedforward_terms.astype(jnp.bfloat16), "narrow").astype(jnp.float32)
    ).astype(jnp.bfloat16)
    cotangent_float = cotangent.astype(jnp.float32)
    shrink_grad = jnp.einsum("tf,td->fd", hidden, cotangent, preferred_element_type=jnp.float32)
    d_hidden = jnp.einsum("td,fd->tf", cotangent, shrink_all, preferred_element_type=jnp.float32)
    d_gate = gelu_pull(d_hidden * up_pre)[0]
    d_up = d_hidden * activated
    d_gate_up = jnp.concatenate([d_gate, d_up], axis=1).astype(jnp.bfloat16)
    expand_grad = jnp.einsum("td,tf->df", normed_two, d_gate_up, preferred_element_type=jnp.float32)
    expand_grad = expand_grad.reshape(model_width, 2, hidden_local).transpose(1, 0, 2)
    second_terms = jnp.einsum(
        "tf,df->td", d_gate_up, expand_flat, preferred_element_type=jnp.float32
    )
    d_normed_two = lax.psum(second_terms, "narrow")
    gain_two_grad = jnp.sum(d_normed_two * middle * scale_two, axis=0)
    d_middle = cotangent_float + norm_back(middle, scale_two, gain_two, d_normed_two)
    d_middle_low = d_middle.astype(jnp.bfloat16)
    output_grad = jnp.einsum(
        "th,td->hd", attended, d_middle_low, preferred_element_type=jnp.float32
    )
    d_attended = jnp.einsum(
        "td,hd->th", d_middle_low, output_all, preferred_element_type=jnp.float32
    ).astype(jnp.bfloat16)

    def buffer_backward(block_items):
        block_rows, segment_row, log_row, grad_rows = block_items
        pieces = split_heads(block_rows)
        same_segment = segment_row[:, None] == segment_row[None, :]
        grad_heads = grad_rows.reshape(length, heads_local, DH).transpose(1, 0, 2)

        def head_backward(head_items):
            query_rows, key_rows, value_rows, bias_row, log_head, grad_head = head_items
            scores = head_scores(query_rows, key_rows, bias_row, same_segment)
            attention_probs = jnp.exp(scores - log_head[:, None])
            grad_probs = jnp.einsum(
                "qd,kd->qk", grad_head, value_rows, preferred_element_type=jnp.float32
            )
            grad_scores = (
                attention_probs
                * (grad_probs - jnp.sum(attention_probs * grad_probs, axis=1, keepdims=True))
            ).astype(jnp.bfloat16)
            grad_query = jnp.dot(grad_scores, key_rows, preferred_element_type=jnp.float32)
            grad_key = jnp.einsum(
                "qk,qd->kd", grad_scores, query_rows, preferred_element_type=jnp.float32
            )
            grad_value = jnp.einsum(
                "qk,qd->kd",
                attention_probs.astype(jnp.bfloat16),
                grad_head,
                preferred_element_type=jnp.float32,
            )
            grad_bias = diagonal_sums(grad_scores.astype(jnp.float32), length)
            return (jnp.stack([grad_query, grad_key, grad_value]).astype(jnp.bfloat16), grad_bias)

        grad_pieces, grad_biases = lax.map(
            head_backward, (pieces[0], pieces[1], pieces[2], head_bias, log_row, grad_heads)
        )
        return (grad_pieces.transpose(2, 1, 0, 3).reshape(length, 3 * head_width), grad_biases)

    grad_qkv, bias_rows = lax.map(
        buffer_backward,
        (buffer_rows, segment_ids, log_totals, d_attended.reshape(buffers, length, head_width)),
    )
    grad_qkv = grad_qkv.reshape(tokens, 3 * head_width)
    project_grad = jnp.einsum("td,tc->dc", normed_one, grad_qkv, preferred_element_type=jnp.float32)
    project_grad = project_grad.reshape(model_width, 3, head_width).transpose(1, 0, 2)
    first_terms = jnp.einsum(
        "tc,dc->td", grad_qkv, project_flat, preferred_element_type=jnp.float32
    )
    d_normed_one = lax.psum(first_terms, "narrow")
    gain_one_grad = jnp.sum(d_normed_one * input_float * scale_one, axis=0)
    input_gradient = (d_middle + norm_back(input_float, scale_one, gain_one, d_normed_one)).astype(
        jnp.bfloat16
    )
    local_bucket = jnp.einsum(
        "hr,rb->bh", jnp.sum(bias_rows, axis=0), onehot, precision=lax.Precision.HIGHEST
    )
    bucket_full = lax.dynamic_update_slice(
        jnp.zeros(bucket_bias.shape, jnp.float32), local_bucket, (jnp.int32(0), head_start)
    )
    project_red, output_red, expand_red, shrink_red, gains_red = (
        lax.psum_scatter(project_grad, "wide", scatter_dimension=1, tiled=True),
        lax.psum_scatter(output_grad, "wide", scatter_dimension=1, tiled=True),
        lax.psum_scatter(expand_grad, "wide", scatter_dimension=1, tiled=True),
        lax.psum_scatter(shrink_grad, "wide", scatter_dimension=1, tiled=True),
        lax.psum_scatter(
            jnp.stack([gain_one_grad, gain_two_grad]), "wide", scatter_dimension=1, tiled=True
        ),
    )
    square_sum = sum(
        (
            jnp.sum(part_grad * part_grad)
            for part_grad in (project_red, output_red, expand_red, shrink_red)
        )
    )
    square_sum = square_sum + jnp.where(
        lax.axis_index("narrow") == 0, jnp.sum(gains_red * gains_red), 0.0
    )
    square_total, bucket_grad = lax.psum((square_sum, bucket_full), ("wide", "narrow"))
    global_norm = jnp.sqrt(square_total + jnp.sum(bucket_grad * bucket_grad))
    factor = jnp.minimum(1.0, clip_limit / (global_norm + 1e-06))
    params = (project_weight, output_weight, expand_weight, shrink_weight, bucket_bias, norm_gains)
    firsts = (project_first, output_first, expand_first, shrink_first, bucket_first, gains_first)
    seconds = (
        project_second,
        output_second,
        expand_second,
        shrink_second,
        bucket_second,
        gains_second,
    )
    reduced = (project_red, output_red, expand_red, shrink_red, bucket_grad, gains_red)
    results = [
        adam_update(weight, moment_one, moment_two, factor * gradient, step_rate, decay_rate)
        for weight, moment_one, moment_two, gradient, step_rate, decay_rate in zip(
            params, firsts, seconds, reduced, step_rates, decay_rates
        )
    ]
    return (
        block_output,
        input_gradient,
        global_norm,
        results[0][0],
        results[1][0],
        results[2][0],
        results[3][0],
        results[4][0],
        results[5][0],
        results[0][1],
        results[1][1],
        results[2][1],
        results[3][1],
        results[4][1],
        results[5][1],
        results[0][2],
        results[1][2],
        results[2][2],
        results[3][2],
        results[4][2],
        results[5][2],
    )


def solution(mesh):
    in_specs = (
        P("wide", None),
        P("wide", None),
        P("wide", None),
        P(None, "wide", "narrow"),
        P("narrow", "wide"),
        P(None, "wide", "narrow"),
        P("narrow", "wide"),
        P(),
        P(None, "wide"),
        P(None, "wide", "narrow"),
        P("narrow", "wide"),
        P(None, "wide", "narrow"),
        P("narrow", "wide"),
        P(),
        P(None, "wide"),
        P(None, "wide", "narrow"),
        P("narrow", "wide"),
        P(None, "wide", "narrow"),
        P("narrow", "wide"),
        P(),
        P(None, "wide"),
    )
    out_specs = (
        P("wide", None),
        P("wide", None),
        P(),
        P(None, "wide", "narrow"),
        P("narrow", "wide"),
        P(None, "wide", "narrow"),
        P("narrow", "wide"),
        P(),
        P(None, "wide"),
        P(None, "wide", "narrow"),
        P("narrow", "wide"),
        P(None, "wide", "narrow"),
        P("narrow", "wide"),
        P(),
        P(None, "wide"),
        P(None, "wide", "narrow"),
        P("narrow", "wide"),
        P(None, "wide", "narrow"),
        P("narrow", "wide"),
        P(),
        P(None, "wide"),
    )
    return jax.shard_map(body, mesh=mesh, in_specs=in_specs, out_specs=out_specs, check_vma=False)
```

profile of v0, /device:TPU:0, one launch (start us, length us, event | category | flops | bytes accessed | tf_op | source)
XLA Modules:
  0.0 1326.2 jit_solution(2225824823571973719)
XLA Ops:
  9.7 22.1 %all-gather = bf16[8,96,2]{1,2,0:T(2,128)(2,1)S(1)} all-gather(bf16[1,96,2]{1,2,0:T(2,128)(2,1)S(1)} %convert_bitcast_fusion), channel_id=1, replica_groups=mesh['wide'=8,'narrow'=4] {'wide'}, dimensions={0}, use_global_device_ids=true | all-gather | bytes 3456 | tf_op jit(solution)/shard_map/all_gather | solution.py:93
  38.3 33.1 %all_gather.17 = bf16[192,768]{0,1:T(8,128)(2,1)} all-gather(bf16[192,96]{0,1:T(8,128)(2,1)S(1)} %copy.186), channel_id=1, replica_groups=mesh['wide'=8,'narrow'=4] {'wide'}, dimensions={1}, use_global_device_ids=true | all-gather | bytes 331776 | tf_op jit(solution)/shard_map/all_gather | solution.py:90
  71.5 35.7 %all_gather.16 = bf16[3,768,192]{2,0,1:T(4,128)(2,1)} all-gather(bf16[3,96,192]{2,0,1:T(4,128)(2,1)S(1)} %copy.181), channel_id=1, replica_groups=mesh['wide'=8,'narrow'=4] {'wide'}, dimensions={1}, use_global_device_ids=true | all-gather | bytes 995328 | tf_op jit(solution)/shard_map/all_gather | solution.py:89
  114.7 152.8 %while.65 = (s32[]{:T(128)}, bf16[2,768,192]{1,2,0:T(8,128)(2,1)}, f32[2,3,768]{2,1,0:T(4,128)}, bf16[2,768,576]{1,2,0:T(8,128)(2,1)}, s32[2,768]{1,0:T(2,128)},...) while((s32[]{:T(128)}, bf16[2,768,192]{1,2,0:T(8,128)(2,1)}, ...), condition=%wide.region_8.9_spmd, body=%wide.region_3.8_spmd.sunk | while | flops 155763456 | bytes 47086936 | solution.py:145
  116.7 73.0 %while.68 = (s32[]{:T(128)}, bf16[3,768,64]{1,2,0:T(8,128)(2,1)S(1)}, f32[3,768]{1,0:T(4,128)S(1)}, bf16[3,768,64]{1,2,0:T(8,128)(2,1)S(1)}, bf16[3,768,64]{1,2,...) while((s32[]{:T(128)}, ...), condition=%wide.region_7.7_spmd.clone, body=%wide.region_4.6_spmd.clone.sunk | while | flops 155763456 | bytes 42930292 | solution.py:142
  120.3 5.6 tile.35
  125.9 7.7 reshape.316
  144.7 5.6 tile.35
  150.3 7.7 reshape.316
  169.0 5.6 tile.35
  174.6 7.7 reshape.316
  193.1 73.0 %while.68 = (s32[]{:T(128)}, bf16[3,768,64]{1,2,0:T(8,128)(2,1)S(1)}, f32[3,768]{1,0:T(4,128)S(1)}, bf16[3,768,64]{1,2,0:T(8,128)(2,1)S(1)}, bf16[3,768,64]{1,2,...) while((s32[]{:T(128)}, ...), condition=%wide.region_7.7_spmd.clone, body=%wide.region_4.6_spmd.clone.sunk | while | flops 155763456 | bytes 42930292 | solution.py:142
  196.7 5.6 tile.35
  202.3 7.7 reshape.316
  221.1 5.6 tile.35
  226.7 7.7 reshape.316
  245.4 5.6 tile.35
  251.0 7.7 reshape.316
  275.6 33.7 %all_gather.19 = bf16[512,768]{0,1:T(8,128)(2,1)S(1)} all-gather(bf16[512,96]{0,1:T(8,128)(2,1)S(1)} %convert_element_type.180), channel_id=1, replica_groups=mesh['wide'=8,'narrow'=4] {'wide'}, dimensions={1}, use_global_device_ids=true | all-gather | bytes 884736 | tf_op jit(solution)/shard_map/all_gather | solution.py:92
  309.3 57.1 %all-reduce.8.cloned.1.call-done = f32[1536,768]{1,0:T(8,128)} async-done(((f32[1536,768]{1,0:T(8,128)}), f32[1536,768]{1,0:T(8,128)}) %all-reduce.8.cloned.1.call-update) | async-done | bytes 4718608 | tf_op jit(solution)/shard_map/psum | solution.py:148
  366.3 5.2 multiply_reduce_fusion.3
  371.6 4.9 copy.188
  376.5 5.4 fusion.103
  381.9 4.7 fusion.64
  397.1 89.9 %all-reduce.12.cloned.1.call-done = f32[1536,768]{1,0:T(8,128)} async-done(((f32[1536,768]{1,0:T(8,128)}), f32[1536,768]{1,0:T(8,128)}) %all-reduce.12.cloned.1.call-update) | async-done | bytes 4718608 | tf_op jit(solution)/shard_map/psum | solution.py:174
  487.1 5.1 multiply_reduce_fusion.1
  492.1 53.7 %all-reduce.10.cloned.1.call-done = bf16[1536,768]{1,0:T(8,128)(2,1)} async-done(((bf16[1536,768]{1,0:T(8,128)(2,1)}), bf16[1536,768]{1,0:T(8,128)(2,1)}) %all-reduce.10.cloned.1.call-update) | async-done | bytes 2359312 | tf_op jit(solution)/shard_map/psum | solution.py:161
  545.9 6.3 subtract_add_fusion
  554.5 346.3 %while.67 = (s32[]{:T(128)}, bf16[2,768,576]{1,2,0:T(8,128)(2,1)}, f32[2,3,1535]{2,1,0:T(4,128)}, bf16[2,768,576]{1,2,0:T(8,128)(2,1)}, f32[2,3,768]{2,1,0:T(4,1...) while((s32[]{:T(128)}, bf16[2,768,576]{1,2,0:T(8,128)(2,1)}, ...), condition=%wide.region_19.20_spmd, body=%wide.region_14.19_spmd.sunk | while | flops 386777856 | bytes 102011568 | solution.py:220
  559.0 165.0 %while.69 = (s32[]{:T(128)}, bf16[3,3,768,64]{2,3,0,1:T(8,128)(2,1)}, f32[3,1535]{1,0:T(4,128)}, bf16[3,768,64]{1,2,0:T(8,128)(2,1)S(1)}, bf16[3,768,64]{1,2,0:T...) while((s32[]{:T(128)}, ...), condition=%wide.region_18.18_spmd.clone, body=%wide.region_15.17_spmd.clone.sunk | while | flops 386777856 | bytes 96039304 | solution.py:215
  564.0 5.6 tile.33
  569.6 7.7 reshape.313
  594.6 4.6 reshape.314
  601.6 8.2 reshape.315
  619.0 5.6 tile.33
  624.6 7.7 reshape.313
  649.6 4.6 reshape.314
  656.6 8.2 reshape.315
  674.0 5.6 tile.33
  679.6 7.7 reshape.313
  704.6 4.6 reshape.314
  711.6 8.2 reshape.315
  731.9 165.0 %while.69 = (s32[]{:T(128)}, bf16[3,3,768,64]{2,3,0,1:T(8,128)(2,1)}, f32[3,1535]{1,0:T(4,128)}, bf16[3,768,64]{1,2,0:T(8,128)(2,1)S(1)}, bf16[3,768,64]{1,2,0:T...) while((s32[]{:T(128)}, ...), condition=%wide.region_18.18_spmd.clone, body=%wide.region_15.17_spmd.clone.sunk | while | flops 386777856 | bytes 96039304 | solution.py:215
  736.8 5.6 tile.33
  742.4 7.7 reshape.313
  767.5 4.6 reshape.314
  774.4 8.2 reshape.315
  791.8 5.6 tile.33
  797.4 7.7 reshape.313
  822.5 4.6 reshape.314
  829.4 8.2 reshape.315
  846.8 5.6 tile.33
  852.4 7.7 reshape.313
  877.5 4.6 reshape.314
  884.4 8.2 reshape.315
  918.4 83.8 %all-reduce.14.cloned.1.call-done = f32[1536,768]{1,0:T(8,128)} async-done(((f32[1536,768]{1,0:T(8,128)}), f32[1536,768]{1,0:T(8,128)}) %all-reduce.14.cloned.1.call-update) | async-done | bytes 4718608 | tf_op jit(solution)/shard_map/psum | solution.py:230
  1015.8 4.7 reshape.293
  1020.7 6.3 fusion.67
  1035.1 8.6 reduce-scatter.18.cloned.1.call-done
  1045.3 62.9 %reduce-scatter.20.cloned.1.call-done = f32[96,2]{1,0:T(8,128)} async-done(((f32[768,2]{1,0:T(8,128)}), f32[96,2]{1,0:T(8,128)}) %reduce-scatter.20.cloned.1.call-update) | async-done | bytes 784
  1110.3 68.5 %reduce-scatter.16.cloned.1.call-done = f32[96,576]{1,0:T(8,128)} async-done(((f32[768,576]{1,0:T(8,128)}), f32[96,576]{1,0:T(8,128)}) %reduce-scatter.16.cloned.1.call-update) | async-done | bytes 221200
  1182.1 73.7 %reduce-scatter.12.cloned.1.call-done = f32[2,96,512]{2,1,0:T(8,128)} async-done(((f32[2,768,512]{2,1,0:T(8,128)}), f32[2,96,512]{2,1,0:T(8,128)}) %reduce-scatter.12.cloned.1.call-update) | async-done | bytes 393232 | tf_op jit(solution)/shard_map/reduce_scatter | solution.py:244
  1258.9 5.5 fusion.54
  1264.5 39.9 %all-reduce.2 = (f32[]{:T(128)}, f32[32,12]{0,1:T(8,128)S(1)}) all-reduce(f32[]{:T(128)S(6)} %add.321, f32[32,12]{0,1:T(8,128)S(1)} %dynamic_update_slice.47), channel_id=1, replica_groups=mesh['wide'=8,'narrow'=4] {'wide','narrow'}, use_global_device_ids=true, to_apply=%region_34.35 | all-reduce | flops 385 | bytes 3080 | tf_op jit(solution)/shard_map/psum | solution.py:259
  (486 shorter events, 355.3 us)
Async XLA Ops:
  8.0 358.3 %all-reduce.8.cloned.1.call-start = ((), (), s32[]{:S(2)}) async-start(), calls=%async_computation.5 | async-start | bytes 9437184 | tf_op jit(solution)/shard_map/psum | solution.py:148
  8.1 104.7 %copy-start.46 = (s32[1535]{0:T(1024)}, s32[1535]{0:T(1024)S(1)}, u32[]{:S(2)}) copy-start(s32[1535]{0:T(1024)S(1)} %fusion.86) | copy-start | bytes 18424
  32.5 77.3 %copy-start.39 = (f32[768]{0:T(1024)}, f32[768]{0:T(1024)S(1)}, u32[]{:S(2)}) copy-start(f32[768]{0:T(1024)S(1)} %get-tuple-element.696) | copy-start | bytes 9220
  35.5 74.3 %copy-start.9 = (bf16[1536,768]{1,0:T(8,128)(2,1)S(1)}, bf16[1536,768]{1,0:T(8,128)(2,1)}, u32[]{:S(2)}) copy-start(bf16[1536,768]{1,0:T(8,128)(2,1)} %param.29) | copy-start | bytes 7077892
  36.1 75.3 %copy-start.34 = (f32[1536]{0:T(1024)}, f32[1536]{0:T(1024)S(1)}, u32[]{:S(2)}) copy-start(f32[1536]{0:T(1024)S(1)} %get-tuple-element.799) | copy-start | bytes 18436
  273.5 92.8 %copy-start.10 = (bf16[1536,768]{1,0:T(8,128)(2,1)S(1)}, bf16[1536,768]{1,0:T(8,128)(2,1)}, u32[]{:S(2)}) copy-start(bf16[1536,768]{1,0:T(8,128)(2,1)} %param.29) | copy-start | bytes 7077892
  273.5 98.0 %all-gather.3.cloned.1.call-start = ((), (), s32[]{:S(2)}) async-start(), calls=%async_computation.6 | async-start | bytes 1769472 | tf_op jit(solution)/shard_map/all_gather | solution.py:91
  275.5 211.6 %all-reduce.12.cloned.1.call-start = ((), (), s32[]{:S(2)}) async-start(), calls=%async_computation.8 | async-start | bytes 9437184 | tf_op jit(solution)/shard_map/psum | solution.py:174
  371.5 4.9 copy-start.41
  371.5 174.3 %copy-start.36 = (f32[1536]{0:T(1024)}, f32[1536]{0:T(1024)S(1)}, u32[]{:S(2)}) copy-start(f32[1536]{0:T(1024)S(1)} %get-tuple-element.801) | copy-start | bytes 18436
  376.5 5.4 copy-start.15
  381.9 6.4 copy-start.18
  392.7 153.1 %all-reduce.10.cloned.1.call-start = ((), (), s32[]{:S(2)}) async-start(), calls=%async_computation.7 | async-start | bytes 4718592 | tf_op jit(solution)/shard_map/psum | solution.py:161
  397.1 605.2 %all-reduce.14.cloned.1.call-start = ((), (), s32[]{:S(2)}) async-start(), calls=%async_computation.9 | async-start | bytes 9437184 | tf_op jit(solution)/shard_map/psum | solution.py:230
  545.9 6.3 copy-start.14
  559.0 4.9 copy-start.4
  559.0 4.9 copy-start.7
  559.1 25.2 %copy-start = (bf16[3,768,64]{1,2,0:T(8,128)(2,1)}, bf16[3,768,64]{1,2,0:T(8,128)(2,1)S(1)}, u32[]{:S(2)}) copy-start(bf16[3,768,64]{1,2,0:T(8,128)(2,1)S(1)} %get-tuple-element.1098) | copy-start | bytes 884740 | tf_op jit(solution)/shard_map/while/body/eval_jaxpr/while
  559.1 25.2 %copy-start.2 = (bf16[3,768,64]{1,2,0:T(8,128)(2,1)}, bf16[3,768,64]{1,2,0:T(8,128)(2,1)S(1)}, u32[]{:S(2)}) copy-start(bf16[3,768,64]{1,2,0:T(8,128)(2,1)S(1)} %get-tuple-element.1097) | copy-start | bytes 884740 | tf_op jit(solution)/shard_map/while/body/eval_jaxpr/while
  614.0 4.9 copy-start.4
  614.1 4.9 copy-start.7
  614.1 25.2 %copy-start = (bf16[3,768,64]{1,2,0:T(8,128)(2,1)}, bf16[3,768,64]{1,2,0:T(8,128)(2,1)S(1)}, u32[]{:S(2)}) copy-start(bf16[3,768,64]{1,2,0:T(8,128)(2,1)S(1)} %get-tuple-element.1098) | copy-start | bytes 884740 | tf_op jit(solution)/shard_map/while/body/eval_jaxpr/while
  614.1 25.2 %copy-start.2 = (bf16[3,768,64]{1,2,0:T(8,128)(2,1)}, bf16[3,768,64]{1,2,0:T(8,128)(2,1)S(1)}, u32[]{:S(2)}) copy-start(bf16[3,768,64]{1,2,0:T(8,128)(2,1)S(1)} %get-tuple-element.1097) | copy-start | bytes 884740 | tf_op jit(solution)/shard_map/while/body/eval_jaxpr/while
  669.0 4.9 copy-start.4
  669.1 4.9 copy-start.7
  669.1 25.2 %copy-start = (bf16[3,768,64]{1,2,0:T(8,128)(2,1)}, bf16[3,768,64]{1,2,0:T(8,128)(2,1)S(1)}, u32[]{:S(2)}) copy-start(bf16[3,768,64]{1,2,0:T(8,128)(2,1)S(1)} %get-tuple-element.1098) | copy-start | bytes 884740 | tf_op jit(solution)/shard_map/while/body/eval_jaxpr/while
  669.1 25.2 %copy-start.2 = (bf16[3,768,64]{1,2,0:T(8,128)(2,1)}, bf16[3,768,64]{1,2,0:T(8,128)(2,1)S(1)}, u32[]{:S(2)}) copy-start(bf16[3,768,64]{1,2,0:T(8,128)(2,1)S(1)} %get-tuple-element.1097) | copy-start | bytes 884740 | tf_op jit(solution)/shard_map/while/body/eval_jaxpr/while
  731.9 4.9 copy-start.4
  731.9 4.9 copy-start.7
  731.9 25.2 %copy-start = (bf16[3,768,64]{1,2,0:T(8,128)(2,1)}, bf16[3,768,64]{1,2,0:T(8,128)(2,1)S(1)}, u32[]{:S(2)}) copy-start(bf16[3,768,64]{1,2,0:T(8,128)(2,1)S(1)} %get-tuple-element.1098) | copy-start | bytes 884740 | tf_op jit(solution)/shard_map/while/body/eval_jaxpr/while
  731.9 25.2 %copy-start.2 = (bf16[3,768,64]{1,2,0:T(8,128)(2,1)}, bf16[3,768,64]{1,2,0:T(8,128)(2,1)S(1)}, u32[]{:S(2)}) copy-start(bf16[3,768,64]{1,2,0:T(8,128)(2,1)S(1)} %get-tuple-element.1097) | copy-start | bytes 884740 | tf_op jit(solution)/shard_map/while/body/eval_jaxpr/while
  786.9 4.9 copy-start.4
  786.9 4.9 copy-start.7
  786.9 25.2 %copy-start = (bf16[3,768,64]{1,2,0:T(8,128)(2,1)}, bf16[3,768,64]{1,2,0:T(8,128)(2,1)S(1)}, u32[]{:S(2)}) copy-start(bf16[3,768,64]{1,2,0:T(8,128)(2,1)S(1)} %get-tuple-element.1098) | copy-start | bytes 884740 | tf_op jit(solution)/shard_map/while/body/eval_jaxpr/while
  786.9 25.2 %copy-start.2 = (bf16[3,768,64]{1,2,0:T(8,128)(2,1)}, bf16[3,768,64]{1,2,0:T(8,128)(2,1)S(1)}, u32[]{:S(2)}) copy-start(bf16[3,768,64]{1,2,0:T(8,128)(2,1)S(1)} %get-tuple-element.1097) | copy-start | bytes 884740 | tf_op jit(solution)/shard_map/while/body/eval_jaxpr/while
  837.6 4.3 copy-start.8
  841.9 4.9 copy-start.4
  841.9 4.9 copy-start.7
  841.9 25.2 %copy-start = (bf16[3,768,64]{1,2,0:T(8,128)(2,1)}, bf16[3,768,64]{1,2,0:T(8,128)(2,1)S(1)}, u32[]{:S(2)}) copy-start(bf16[3,768,64]{1,2,0:T(8,128)(2,1)S(1)} %get-tuple-element.1098) | copy-start | bytes 884740 | tf_op jit(solution)/shard_map/while/body/eval_jaxpr/while
  841.9 25.2 %copy-start.2 = (bf16[3,768,64]{1,2,0:T(8,128)(2,1)}, bf16[3,768,64]{1,2,0:T(8,128)(2,1)S(1)}, u32[]{:S(2)}) copy-start(bf16[3,768,64]{1,2,0:T(8,128)(2,1)S(1)} %get-tuple-element.1097) | copy-start | bytes 884740 | tf_op jit(solution)/shard_map/while/body/eval_jaxpr/while
  908.0 5.7 copy-start.13
  908.0 125.5 %reduce-scatter.14.cloned.1.call-start = ((), (), s32[]{:S(2)}) async-start(), calls=%async_computation.11 | async-start | bytes 1769472 | tf_op jit(solution)/shard_map/reduce_scatter | solution.py:245
  913.6 4.8 copy-start.44
  913.6 88.6 %copy-start.11 = (bf16[1536,768]{1,0:T(8,128)(2,1)S(1)}, bf16[1536,768]{1,0:T(8,128)(2,1)}, u32[]{:S(2)}) copy-start(bf16[1536,768]{1,0:T(8,128)(2,1)} %param.29) | copy-start | bytes 7077892
  913.6 88.6 %copy-start.35 = (f32[1536]{0:T(1024)S(1)}, f32[1536]{0:T(1024)}, u32[]{:S(2)}) copy-start(f32[1536]{0:T(1024)} %copy-done.34) | copy-start | bytes 18436
  913.7 88.6 %copy-start.40 = (f32[768]{0:T(1024)S(1)}, f32[768]{0:T(1024)}, u32[]{:S(2)}) copy-start(f32[768]{0:T(1024)} %copy-done.39) | copy-start | bytes 9220
  913.7 130.1 %reduce-scatter.18.cloned.1.call-start = ((), (), s32[]{:S(2)}) async-start(), calls=%async_computation.13 | async-start | bytes 884736
  918.3 189.9 %reduce-scatter.20.cloned.1.call-start = ((), (), s32[]{:S(2)}) async-start(), calls=%async_computation.14 | async-start | bytes 442368
  1007.0 171.8 %reduce-scatter.16.cloned.1.call-start = ((), (), s32[]{:S(2)}) async-start(), calls=%async_computation.12 | async-start | bytes 2211840
  1015.8 4.9 copy-start.37
  1015.8 4.9 copy-start.42
  1020.5 235.4 %reduce-scatter.12.cloned.1.call-start = ((), (), s32[]{:S(2)}) async-start(), calls=%async_computation.10 | async-start | bytes 3538944 | tf_op jit(solution)/shard_map/reduce_scatter | solution.py:244
  1029.0 229.9 %copy-start.43 = (f32[1536]{0:T(1024)S(1)}, f32[1536]{0:T(1024)}, u32[]{:S(2)}) copy-start(f32[1536]{0:T(1024)} %get-tuple-element.798) | copy-start | bytes 18436
  1109.1 149.8 %copy-start.48 = (f32[2,96]{1,0:T(2,128)}, f32[2,96]{1,0:T(2,128)S(1)}, u32[]{:S(2)}) copy-start(f32[2,96]{1,0:T(2,128)S(1)} %copy.205) | copy-start | bytes 2308
  1258.9 47.5 %copy-start.22 = (f32[3,96,192]{1,2,0:T(8,128)S(1)}, f32[3,96,192]{1,2,0:T(8,128)}, u32[]{:S(2)}) copy-start(f32[3,96,192]{1,2,0:T(8,128)} %copy.193) | copy-start | bytes 663556
  1264.4 48.4 %copy-start.29 = (f32[192,96]{1,0:T(8,128)S(1)}, f32[192,96]{1,0:T(8,128)}, u32[]{:S(2)}) copy-start(f32[192,96]{1,0:T(8,128)} %param.33) | copy-start | bytes 221188
  1264.4 48.4 %copy-start.32 = (f32[192,96]{1,0:T(8,128)S(1)}, f32[192,96]{1,0:T(8,128)}, u32[]{:S(2)}) copy-start(f32[192,96]{1,0:T(8,128)} %param.39) | copy-start | bytes 221188
  1264.4 48.4 %copy-start.33 = (f32[192,96]{1,0:T(8,128)S(1)}, f32[192,96]{1,0:T(8,128)}, u32[]{:S(2)}) copy-start(f32[192,96]{1,0:T(8,128)} %param.45) | copy-start | bytes 221188
  1264.4 49.2 %copy-start.27 = (f32[512,96]{0,1:T(8,128)S(1)}, f32[512,96]{0,1:T(8,128)}, u32[]{:S(2)}) copy-start(f32[512,96]{0,1:T(8,128)} %param.35) | copy-start | bytes 589828
  1264.4 49.2 %copy-start.28 = (f32[512,96]{0,1:T(8,128)S(1)}, f32[512,96]{0,1:T(8,128)}, u32[]{:S(2)}) copy-start(f32[512,96]{0,1:T(8,128)} %reduce-scatter.14.cloned.1.call-done) | copy-start | bytes 589828
  1264.4 49.2 %copy-start.31 = (f32[512,96]{0,1:T(8,128)S(1)}, f32[512,96]{0,1:T(8,128)}, u32[]{:S(2)}) copy-start(f32[512,96]{0,1:T(8,128)} %param.41) | copy-start | bytes 589828
  1264.5 51.0 %copy-start.20 = (f32[2,96,512]{2,1,0:T(8,128)S(1)}, f32[2,96,512]{2,1,0:T(8,128)}, u32[]{:S(2)}) copy-start(f32[2,96,512]{2,1,0:T(8,128)} %param.34) | copy-start | bytes 1179652
  1264.5 51.0 %copy-start.21 = (f32[2,96,512]{2,1,0:T(8,128)S(1)}, f32[2,96,512]{2,1,0:T(8,128)}, u32[]{:S(2)}) copy-start(f32[2,96,512]{2,1,0:T(8,128)} %reduce-scatter.12.cloned.1.call-done) | copy-start | bytes 1179652
  1304.4 7.1 copy-start.45
  (37 other events, 124.1 us)
Sparse Core Ops, SparseCore 0:
  273.6 92.6 all-reduce.7
  392.9 94.1 all-reduce.11
  490.0 55.8 all-reduce.9
  908.1 94.1 all-reduce.13
Sparse Core Ops, SparseCore 1:
  276.8 43.9 all-gather.2
  913.7 65.1 reduce-scatter.13
  982.4 61.3 reduce-scatter.17
  1047.6 60.6 reduce-scatter.19
  1112.3 66.5 reduce-scatter.15
  1182.9 72.9 reduce-scatter.11
where the time goes:
time: 1340 us; the launch traced here: 1330 us
  waiting for transfers between devices  498 us (37%)
  local copies, waits for them, and re-layouts  451 us (34%)
  blocking collectives  165 us (12%)
  matrix products  99.9 us (7%)
  other arithmetic  88 us (7%)
  between operations  21.8 us (2%)
    unnamed x13, waiting for transfers between devices  140 us
    another operation x24, local copies, waits for them, and re-layouts, toeplitz_rows(): tiled_flat = jnp.tile(padded, length)[:length * (2 * length - 1)]  100 us
    reshape x12, local copies, waits for them, and re-layouts, toeplitz_rows(): return tiled_flat.reshape(length, 2 * length - 1)[:, length - 1:]  92.6 us
    psum x1, waiting for transfers between devices, body(): d_normed_two = lax.psum(second_terms, 'narrow')  89.9 us
    psum x1, waiting for transfers between devices, body(): d_normed_one = lax.psum(first_terms, 'narrow')  83.8 us
    reduce_scatter x1, waiting for transfers between devices, body(): lax.psum_scatter(expand_grad, 'wide', scatter_dimension=1, tiled=True)  73.7 us
    psum x1, waiting for transfers between devices, body(): middle = input_float + lax.psum(attention_terms, 'narrow')  57.1 us
    psum x1, waiting for transfers between devices, body(): lax.psum(feedforward_terms.astype(jnp.bfloat16), 'narrow')  53.7 us
  transfers between devices with their start and end apart: 10, of which 8 were waited for; matrix products, arithmetic and copies ran while one was open for 5% of the time, Pallas kernels for 0%

commit v1 on v0

--- a/solution.py
+++ b/solution.py
@@ -145,7 +145,7 @@
     attended, log_totals = lax.map(buffer_forward, (buffer_rows, segment_ids))
     attended = attended.reshape(tokens, head_width)
     attention_terms = jnp.dot(attended, output_all, preferred_element_type=jnp.float32)
-    middle = input_float + lax.psum(attention_terms, "narrow")
+    middle = input_float + jnp.sum(lax.all_gather(attention_terms, "narrow"), axis=0)
     scale_two = rms_scale(middle)
     normed_two = (middle * scale_two * gain_two).astype(jnp.bfloat16)
     expand_flat = jnp.transpose(expand_all, (1, 0, 2)).reshape(model_width, 2 * hidden_local)

time: 1340 us -> 1460 us (1.090)
  waiting for transfers between devices: 498 us -> 614 us
    all_gather x0 -> x1, waiting for transfers between devices: none -> 81.9 us  [body(): lax.all_gather(attention_terms, 'narrow')]
    psum x1 -> x0, waiting for transfers between devices: 57.1 us -> none  [body(): middle = input_float + lax.psum(attention_terms, 'narrow')]
    unnamed x13, waiting for transfers between devices: 140 us -> 194 us
    reduce_scatter x1, waiting for transfers between devices: 0.03 us -> 37.1 us  [body(): lax.psum_scatter(shrink_grad, 'wide', scatter_dimension=1, tiled=True)]
  transfers between devices with their start and end apart: 10 -> 10, of which waited for: 8 -> 9; matrix products, arithmetic and copies ran while one was open for 5% -> 16% of each run, Pallas kernels for 0% -> 0%
where the time goes in v1:
time: 1460 us; the launch traced here: 1450 us
  waiting for transfers between devices  614 us (42%)
  local copies, waits for them, and re-layouts  451 us (31%)
  blocking collectives  168 us (12%)
  other arithmetic  96.4 us (7%)
  matrix products  96.3 us (7%)
  between operations  20.7 us (1%)
    unnamed x13, waiting for transfers between devices  194 us
    another operation x24, local copies, waits for them, and re-layouts, toeplitz_rows(): tiled_flat = jnp.tile(padded, length)[:length * (2 * length - 1)]  100 us
    reshape x12, local copies, waits for them, and re-layouts, toeplitz_rows(): return tiled_flat.reshape(length, 2 * length - 1)[:, length - 1:]  92.6 us
    psum x1, waiting for transfers between devices, body(): d_normed_two = lax.psum(second_terms, 'narrow')  89.8 us
    psum x1, waiting for transfers between devices, body(): d_normed_one = lax.psum(first_terms, 'narrow')  83.8 us
    all_gather x1, waiting for transfers between devices, body(): lax.all_gather(attention_terms, 'narrow')  81.9 us
    reduce_scatter x1, waiting for transfers between devices, body(): lax.psum_scatter(expand_grad, 'wide', scatter_dimension=1, tiled=True)  73.8 us
    psum x1, waiting for transfers between devices, body(): lax.psum(feedforward_terms.astype(jnp.bfloat16), 'narrow')  53.6 us
  transfers between devices with their start and end apart: 10, of which 9 were waited for; matrix products, arithmetic and copies ran while one was open for 16% of the time, Pallas kernels for 0%

profile of v1, /device:TPU:0, one launch (start us, length us, event | category | flops | bytes accessed | tf_op | source)
XLA Modules:
  0.0 1449.0 jit_solution(10481369356298266114)
XLA Ops:
  10.9 22.1 %all-gather.1 = bf16[8,96,2]{1,2,0:T(2,128)(2,1)S(1)} all-gather(bf16[1,96,2]{1,2,0:T(2,128)(2,1)S(1)} %convert_bitcast_fusion), channel_id=1, replica_groups=mesh['wide'=8,'narrow'=4] {'wide'}, dimensions={0}, use_global_device_ids=true | all-gather | bytes 3456 | tf_op jit(solution)/shard_map/all_gather | solution.py:93
  37.7 43.0 %all_gather.22 = bf16[3,768,192]{2,0,1:T(4,128)(2,1)} all-gather(bf16[3,96,192]{2,0,1:T(4,128)(2,1)S(1)} %copy.181), channel_id=1, replica_groups=mesh['wide'=8,'narrow'=4] {'wide'}, dimensions={1}, use_global_device_ids=true | all-gather | bytes 995328 | tf_op jit(solution)/shard_map/all_gather | solution.py:89
  88.3 152.8 %while.65 = (s32[]{:T(128)}, bf16[2,768,192]{1,2,0:T(8,128)(2,1)}, f32[2,3,768]{2,1,0:T(4,128)}, bf16[2,768,576]{1,2,0:T(8,128)(2,1)}, s32[2,768]{1,0:T(2,128)},...) while((s32[]{:T(128)}, bf16[2,768,192]{1,2,0:T(8,128)(2,1)}, ...), condition=%wide.region_8.9_spmd, body=%wide.region_3.8_spmd.sunk | while | flops 155763456 | bytes 47086936 | solution.py:145
  90.3 73.0 %while.68 = (s32[]{:T(128)}, bf16[3,768,64]{1,2,0:T(8,128)(2,1)S(1)}, f32[3,768]{1,0:T(4,128)S(1)}, bf16[3,768,64]{1,2,0:T(8,128)(2,1)S(1)}, bf16[3,768,64]{1,2,...) while((s32[]{:T(128)}, ...), condition=%wide.region_7.7_spmd.clone, body=%wide.region_4.6_spmd.clone.sunk | while | flops 155763456 | bytes 42930292 | solution.py:142
  93.9 5.6 tile.35
  99.5 7.7 reshape.317
  118.3 5.6 tile.35
  123.9 7.7 reshape.317
  142.6 5.6 tile.35
  148.2 7.7 reshape.317
  166.7 73.0 %while.68 = (s32[]{:T(128)}, bf16[3,768,64]{1,2,0:T(8,128)(2,1)S(1)}, f32[3,768]{1,0:T(4,128)S(1)}, bf16[3,768,64]{1,2,0:T(8,128)(2,1)S(1)}, bf16[3,768,64]{1,2,...) while((s32[]{:T(128)}, ...), condition=%wide.region_7.7_spmd.clone, body=%wide.region_4.6_spmd.clone.sunk | while | flops 155763456 | bytes 42930292 | solution.py:142
  170.3 5.6 tile.35
  175.9 7.7 reshape.317
  194.7 5.6 tile.35
  200.3 7.7 reshape.317
  219.0 5.6 tile.35
  224.6 7.7 reshape.317
  243.2 31.1 %all_gather.23 = bf16[192,768]{0,1:T(8,128)(2,1)S(1)} all-gather(bf16[192,96]{0,1:T(8,128)(2,1)S(1)} %copy.186), channel_id=1, replica_groups=mesh['wide'=8,'narrow'=4] {'wide'}, dimensions={1}, use_global_device_ids=true | all-gather | bytes 331776 | tf_op jit(solution)/shard_map/all_gather | solution.py:90
  278.2 32.0 %all_gather.27 = bf16[512,768]{0,1:T(8,128)(2,1)S(1)} all-gather(bf16[512,96]{0,1:T(8,128)(2,1)S(1)} %convert_element_type.180), channel_id=1, replica_groups=mesh['wide'=8,'narrow'=4] {'wide'}, dimensions={1}, use_global_device_ids=true | all-gather | bytes 884736 | tf_op jit(solution)/shard_map/all_gather | solution.py:92
  310.3 4.9 copy.188
  315.2 81.9 %all-gather.7.cloned.1.call-done = f32[6144,768]{1,0:T(8,128)} async-done(((f32[1536,768]{1,0:T(8,128)}), f32[6144,768]{1,0:T(8,128)}) %all-gather.7.cloned.1.call-update) | async-done | bytes 18874384 | tf_op jit(solution)/shard_map/all_gather | solution.py:148
  397.0 10.5 reduce_sum.170
  414.1 4.7 fusion.64
  429.4 89.8 %all-reduce.9.cloned.1.call-done = f32[1536,768]{1,0:T(8,128)} async-done(((f32[1536,768]{1,0:T(8,128)}), f32[1536,768]{1,0:T(8,128)}) %all-reduce.9.cloned.1.call-update) | async-done | bytes 4718608 | tf_op jit(solution)/shard_map/psum | solution.py:174
  519.2 5.1 multiply_reduce_fusion.1
  524.3 53.6 %all-reduce.7.cloned.1.call-done = bf16[1536,768]{1,0:T(8,128)(2,1)} async-done(((bf16[1536,768]{1,0:T(8,128)(2,1)}), bf16[1536,768]{1,0:T(8,128)(2,1)}) %all-reduce.7.cloned.1.call-update) | async-done | bytes 2359312 | tf_op jit(solution)/shard_map/psum | solution.py:161
  577.8 6.2 subtract_add_fusion
  586.5 346.4 %while.67 = (s32[]{:T(128)}, bf16[2,768,576]{1,2,0:T(8,128)(2,1)}, f32[2,3,1535]{2,1,0:T(4,128)}, bf16[2,768,576]{1,2,0:T(8,128)(2,1)}, f32[2,3,768]{2,1,0:T(4,1...) while((s32[]{:T(128)}, bf16[2,768,576]{1,2,0:T(8,128)(2,1)}, ...), condition=%wide.region_19.20_spmd, body=%wide.region_14.19_spmd.sunk | while | flops 386777856 | bytes 102011568 | solution.py:220
  591.0 165.1 %while.69 = (s32[]{:T(128)}, bf16[3,3,768,64]{2,3,0,1:T(8,128)(2,1)}, f32[3,1535]{1,0:T(4,128)}, bf16[3,768,64]{1,2,0:T(8,128)(2,1)S(1)}, bf16[3,768,64]{1,2,0:T...) while((s32[]{:T(128)}, ...), condition=%wide.region_18.18_spmd.clone, body=%wide.region_15.17_spmd.clone.sunk | while | flops 386777856 | bytes 96039304 | solution.py:215
  595.9 5.6 tile.33
  601.5 7.7 reshape.314
  626.6 4.6 reshape.315
  633.6 8.2 reshape.316
  651.0 5.6 tile.33
  656.6 7.7 reshape.314
  681.6 4.6 reshape.315
  688.6 8.2 reshape.316
  706.0 5.6 tile.33
  711.6 7.7 reshape.314
  736.7 4.6 reshape.315
  743.6 8.2 reshape.316
  763.9 165.1 %while.69 = (s32[]{:T(128)}, bf16[3,3,768,64]{2,3,0,1:T(8,128)(2,1)}, f32[3,1535]{1,0:T(4,128)}, bf16[3,768,64]{1,2,0:T(8,128)(2,1)S(1)}, bf16[3,768,64]{1,2,0:T...) while((s32[]{:T(128)}, ...), condition=%wide.region_18.18_spmd.clone, body=%wide.region_15.17_spmd.clone.sunk | while | flops 386777856 | bytes 96039304 | solution.py:215
  768.9 5.6 tile.33
  774.5 7.7 reshape.314
  799.5 4.6 reshape.315
  806.5 8.2 reshape.316
  823.9 5.6 tile.33
  829.5 7.7 reshape.314
  854.6 4.6 reshape.315
  861.5 8.2 reshape.316
  878.9 5.6 tile.33
  884.5 7.7 reshape.314
  909.6 4.6 reshape.315
  916.5 8.2 reshape.316
  950.5 83.8 %all-reduce.11.cloned.1.call-done = f32[1536,768]{1,0:T(8,128)} async-done(((f32[1536,768]{1,0:T(8,128)}), f32[1536,768]{1,0:T(8,128)}) %all-reduce.11.cloned.1.call-update) | async-done | bytes 4718608 | tf_op jit(solution)/shard_map/psum | solution.py:230
  1047.8 4.7 reshape.294
  1052.8 6.3 fusion.67
  1065.6 37.1 %reduce-scatter.14.cloned.1.call-done = f32[512,96]{0,1:T(8,128)} async-done(((f32[512,768]{0,1:T(8,128)}), f32[512,96]{0,1:T(8,128)}) %reduce-scatter.14.cloned.1.call-update) | async-done | bytes 196624 | tf_op jit(solution)/shard_map/reduce_scatter | solution.py:245
  1104.2 63.5 %reduce-scatter.18.cloned.1.call-done = f32[96,192]{1,0:T(8,128)} async-done(((f32[768,192]{1,0:T(8,128)}), f32[96,192]{1,0:T(8,128)}) %reduce-scatter.18.cloned.1.call-update) | async-done | bytes 73744
  1169.3 62.7 %reduce-scatter.20.cloned.1.call-done = f32[96,2]{1,0:T(8,128)} async-done(((f32[768,2]{1,0:T(8,128)}), f32[96,2]{1,0:T(8,128)}) %reduce-scatter.20.cloned.1.call-update) | async-done | bytes 784
  1234.2 67.7 %reduce-scatter.16.cloned.1.call-done = f32[96,576]{1,0:T(8,128)} async-done(((f32[768,576]{1,0:T(8,128)}), f32[96,576]{1,0:T(8,128)}) %reduce-scatter.16.cloned.1.call-update) | async-done | bytes 221200
  1305.1 73.8 %reduce-scatter.12.cloned.1.call-done = f32[2,96,512]{2,1,0:T(8,128)} async-done(((f32[2,768,512]{2,1,0:T(8,128)}), f32[2,96,512]{2,1,0:T(8,128)}) %reduce-scatter.12.cloned.1.call-update) | async-done | bytes 393232 | tf_op jit(solution)/shard_map/reduce_scatter | solution.py:244
  1382.0 5.5 fusion.54
  1387.5 39.9 %all-reduce.2 = (f32[]{:T(128)}, f32[32,12]{0,1:T(8,128)S(1)}) all-reduce(f32[]{:T(128)S(6)} %add.319, f32[32,12]{0,1:T(8,128)S(1)} %dynamic_update_slice.47), channel_id=1, replica_groups=mesh['wide'=8,'narrow'=4] {'wide','narrow'}, use_global_device_ids=true, to_apply=%region_34.35 | all-reduce | flops 385 | bytes 3080 | tf_op jit(solution)/shard_map/psum | solution.py:259
  (489 shorter events, 360.2 us)
Async XLA Ops:
  7.2 30.4 %copy-start.22 = (f32[3,96,192]{2,1,0:T(8,128)S(1)}, f32[3,96,192]{2,1,0:T(8,128)}, u32[]{:S(2)}) copy-start(f32[3,96,192]{2,1,0:T(8,128)} %param.32) | copy-start | bytes 663556
  7.2 303.1 %all-gather.5.cloned.1.call-start = ((), (), s32[]{:S(2)}) async-start(), calls=%async_computation.5 | async-start | bytes 1769472 | tf_op jit(solution)/shard_map/all_gather | solution.py:91
  9.3 387.7 %all-gather.7.cloned.1.call-start = ((), (), s32[]{:S(2)}) async-start(), calls=%async_computation.11 | async-start | bytes 23592960 | tf_op jit(solution)/shard_map/all_gather | solution.py:148
  9.4 77.0 %copy-start.47 = (s32[1535]{0:T(1024)}, s32[1535]{0:T(1024)S(1)}, u32[]{:S(2)}) copy-start(s32[1535]{0:T(1024)S(1)} %fusion.86) | copy-start | bytes 18424
  33.8 49.5 %copy-start.39 = (f32[768]{0:T(1024)}, f32[768]{0:T(1024)S(1)}, u32[]{:S(2)}) copy-start(f32[768]{0:T(1024)S(1)} %get-tuple-element.696) | copy-start | bytes 9220
  34.6 48.7 %copy-start.10 = (bf16[1536,768]{1,0:T(8,128)(2,1)S(1)}, bf16[1536,768]{1,0:T(8,128)(2,1)}, u32[]{:S(2)}) copy-start(bf16[1536,768]{1,0:T(8,128)(2,1)} %param.29) | copy-start | bytes 7077892
  37.6 47.4 %copy-start.34 = (f32[1536]{0:T(1024)}, f32[1536]{0:T(1024)S(1)}, u32[]{:S(2)}) copy-start(f32[1536]{0:T(1024)S(1)} %get-tuple-element.799) | copy-start | bytes 18436
  243.2 31.1 %copy-start.13 = (bf16[2,24,8,768]{3,2,0,1:T(8,128)(2,1)}, bf16[2,24,8,768]{3,2,0,1:T(8,128)(2,1)S(1)}, u32[]{:S(2)}) copy-start(bf16[2,24,8,768]{3,2,0,1:T(8,128)(2,1)S(1)} %copy.221) | copy-start | bytes 1769476
  277.3 241.9 %all-reduce.9.cloned.1.call-start = ((), (), s32[]{:S(2)}) async-start(), calls=%async_computation.7 | async-start | bytes 9437184 | tf_op jit(solution)/shard_map/psum | solution.py:174
  397.0 10.5 copy-start.11
  411.4 166.5 %copy-start.36 = (f32[1536]{0:T(1024)}, f32[1536]{0:T(1024)S(1)}, u32[]{:S(2)}) copy-start(f32[1536]{0:T(1024)S(1)} %get-tuple-element.801) | copy-start | bytes 18436
  425.0 152.8 %all-reduce.7.cloned.1.call-start = ((), (), s32[]{:S(2)}) async-start(), calls=%async_computation.6 | async-start | bytes 4718592 | tf_op jit(solution)/shard_map/psum | solution.py:161
  429.3 605.0 %all-reduce.11.cloned.1.call-start = ((), (), s32[]{:S(2)}) async-start(), calls=%async_computation.8 | async-start | bytes 9437184 | tf_op jit(solution)/shard_map/psum | solution.py:230
  429.4 148.4 %copy-start.44 = (f32[1536]{0:T(1024)S(1)}, f32[1536]{0:T(1024)}, u32[]{:S(2)}) copy-start(f32[1536]{0:T(1024)} %get-tuple-element.800) | copy-start | bytes 18436
  591.0 4.9 copy-start.4
  591.0 4.9 copy-start.7
  591.0 25.2 %copy-start = (bf16[3,768,64]{1,2,0:T(8,128)(2,1)}, bf16[3,768,64]{1,2,0:T(8,128)(2,1)S(1)}, u32[]{:S(2)}) copy-start(bf16[3,768,64]{1,2,0:T(8,128)(2,1)S(1)} %get-tuple-element.1098) | copy-start | bytes 884740 | tf_op jit(solution)/shard_map/while/body/eval_jaxpr/while
  591.0 25.2 %copy-start.2 = (bf16[3,768,64]{1,2,0:T(8,128)(2,1)}, bf16[3,768,64]{1,2,0:T(8,128)(2,1)S(1)}, u32[]{:S(2)}) copy-start(bf16[3,768,64]{1,2,0:T(8,128)(2,1)S(1)} %get-tuple-element.1097) | copy-start | bytes 884740 | tf_op jit(solution)/shard_map/while/body/eval_jaxpr/while
  641.8 4.3 copy-start.8
  646.1 4.9 copy-start.4
  646.1 4.9 copy-start.7
  646.1 25.2 %copy-start = (bf16[3,768,64]{1,2,0:T(8,128)(2,1)}, bf16[3,768,64]{1,2,0:T(8,128)(2,1)S(1)}, u32[]{:S(2)}) copy-start(bf16[3,768,64]{1,2,0:T(8,128)(2,1)S(1)} %get-tuple-element.1098) | copy-start | bytes 884740 | tf_op jit(solution)/shard_map/while/body/eval_jaxpr/while
  646.1 25.2 %copy-start.2 = (bf16[3,768,64]{1,2,0:T(8,128)(2,1)}, bf16[3,768,64]{1,2,0:T(8,128)(2,1)S(1)}, u32[]{:S(2)}) copy-start(bf16[3,768,64]{1,2,0:T(8,128)(2,1)S(1)} %get-tuple-element.1097) | copy-start | bytes 884740 | tf_op jit(solution)/shard_map/while/body/eval_jaxpr/while
  701.1 4.9 copy-start.4
  701.1 4.9 copy-start.7
  701.1 25.2 %copy-start = (bf16[3,768,64]{1,2,0:T(8,128)(2,1)}, bf16[3,768,64]{1,2,0:T(8,128)(2,1)S(1)}, u32[]{:S(2)}) copy-start(bf16[3,768,64]{1,2,0:T(8,128)(2,1)S(1)} %get-tuple-element.1098) | copy-start | bytes 884740 | tf_op jit(solution)/shard_map/while/body/eval_jaxpr/while
  701.1 25.2 %copy-start.2 = (bf16[3,768,64]{1,2,0:T(8,128)(2,1)}, bf16[3,768,64]{1,2,0:T(8,128)(2,1)S(1)}, u32[]{:S(2)}) copy-start(bf16[3,768,64]{1,2,0:T(8,128)(2,1)S(1)} %get-tuple-element.1097) | copy-start | bytes 884740 | tf_op jit(solution)/shard_map/while/body/eval_jaxpr/while
  751.8 4.3 copy-start.8
  763.9 4.9 copy-start.4
  763.9 4.9 copy-start.7
  763.9 25.2 %copy-start = (bf16[3,768,64]{1,2,0:T(8,128)(2,1)}, bf16[3,768,64]{1,2,0:T(8,128)(2,1)S(1)}, u32[]{:S(2)}) copy-start(bf16[3,768,64]{1,2,0:T(8,128)(2,1)S(1)} %get-tuple-element.1098) | copy-start | bytes 884740 | tf_op jit(solution)/shard_map/while/body/eval_jaxpr/while
  764.0 25.2 %copy-start.2 = (bf16[3,768,64]{1,2,0:T(8,128)(2,1)}, bf16[3,768,64]{1,2,0:T(8,128)(2,1)S(1)}, u32[]{:S(2)}) copy-start(bf16[3,768,64]{1,2,0:T(8,128)(2,1)S(1)} %get-tuple-element.1097) | copy-start | bytes 884740 | tf_op jit(solution)/shard_map/while/body/eval_jaxpr/while
  819.0 4.9 copy-start.4
  819.0 4.9 copy-start.7
  819.0 25.2 %copy-start = (bf16[3,768,64]{1,2,0:T(8,128)(2,1)}, bf16[3,768,64]{1,2,0:T(8,128)(2,1)S(1)}, u32[]{:S(2)}) copy-start(bf16[3,768,64]{1,2,0:T(8,128)(2,1)S(1)} %get-tuple-element.1098) | copy-start | bytes 884740 | tf_op jit(solution)/shard_map/while/body/eval_jaxpr/while
  819.0 25.2 %copy-start.2 = (bf16[3,768,64]{1,2,0:T(8,128)(2,1)}, bf16[3,768,64]{1,2,0:T(8,128)(2,1)S(1)}, u32[]{:S(2)}) copy-start(bf16[3,768,64]{1,2,0:T(8,128)(2,1)S(1)} %get-tuple-element.1097) | copy-start | bytes 884740 | tf_op jit(solution)/shard_map/while/body/eval_jaxpr/while
  874.0 4.9 copy-start.4
  874.0 4.9 copy-start.7
  874.0 25.2 %copy-start = (bf16[3,768,64]{1,2,0:T(8,128)(2,1)}, bf16[3,768,64]{1,2,0:T(8,128)(2,1)S(1)}, u32[]{:S(2)}) copy-start(bf16[3,768,64]{1,2,0:T(8,128)(2,1)S(1)} %get-tuple-element.1098) | copy-start | bytes 884740 | tf_op jit(solution)/shard_map/while/body/eval_jaxpr/while
  874.0 25.2 %copy-start.2 = (bf16[3,768,64]{1,2,0:T(8,128)(2,1)}, bf16[3,768,64]{1,2,0:T(8,128)(2,1)S(1)}, u32[]{:S(2)}) copy-start(bf16[3,768,64]{1,2,0:T(8,128)(2,1)S(1)} %get-tuple-element.1097) | copy-start | bytes 884740 | tf_op jit(solution)/shard_map/while/body/eval_jaxpr/while
  940.1 5.7 copy-start.14
  940.1 162.6 %reduce-scatter.14.cloned.1.call-start = ((), (), s32[]{:S(2)}) async-start(), calls=%async_computation.10 | async-start | bytes 1769472 | tf_op jit(solution)/shard_map/reduce_scatter | solution.py:245
  945.7 4.8 copy-start.45
  945.7 88.6 %copy-start.12 = (bf16[1536,768]{1,0:T(8,128)(2,1)S(1)}, bf16[1536,768]{1,0:T(8,128)(2,1)}, u32[]{:S(2)}) copy-start(bf16[1536,768]{1,0:T(8,128)(2,1)} %param.29) | copy-start | bytes 7077892
  945.7 88.6 %copy-start.35 = (f32[1536]{0:T(1024)S(1)}, f32[1536]{0:T(1024)}, u32[]{:S(2)}) copy-start(f32[1536]{0:T(1024)} %copy-done.34) | copy-start | bytes 18436
  945.7 88.6 %copy-start.40 = (f32[768]{0:T(1024)S(1)}, f32[768]{0:T(1024)}, u32[]{:S(2)}) copy-start(f32[768]{0:T(1024)} %copy-done.39) | copy-start | bytes 9220
  945.7 222.0 %reduce-scatter.18.cloned.1.call-start = ((), (), s32[]{:S(2)}) async-start(), calls=%async_computation.13 | async-start | bytes 884736
  950.4 281.6 %reduce-scatter.20.cloned.1.call-start = ((), (), s32[]{:S(2)}) async-start(), calls=%async_computation.14 | async-start | bytes 442368
  1039.1 262.7 %reduce-scatter.16.cloned.1.call-start = ((), (), s32[]{:S(2)}) async-start(), calls=%async_computation.12 | async-start | bytes 2211840
  1047.8 4.9 copy-start.37
  1047.8 4.9 copy-start.42
  1052.5 326.4 %reduce-scatter.12.cloned.1.call-start = ((), (), s32[]{:S(2)}) async-start(), calls=%async_computation.9 | async-start | bytes 3538944 | tf_op jit(solution)/shard_map/reduce_scatter | solution.py:244
  1061.1 320.8 %copy-start.43 = (f32[1536]{0:T(1024)S(1)}, f32[1536]{0:T(1024)}, u32[]{:S(2)}) copy-start(f32[1536]{0:T(1024)} %get-tuple-element.798) | copy-start | bytes 18436
  1232.9 149.0 %copy-start.49 = (f32[2,96]{1,0:T(2,128)}, f32[2,96]{1,0:T(2,128)S(1)}, u32[]{:S(2)}) copy-start(f32[2,96]{1,0:T(2,128)S(1)} %copy.205) | copy-start | bytes 2308
  1381.9 47.4 %copy-start.21 = (f32[3,96,192]{1,2,0:T(8,128)S(1)}, f32[3,96,192]{1,2,0:T(8,128)}, u32[]{:S(2)}) copy-start(f32[3,96,192]{1,2,0:T(8,128)} %copy.193) | copy-start | bytes 663556
  1387.5 48.4 %copy-start.29 = (f32[192,96]{1,0:T(8,128)S(1)}, f32[192,96]{1,0:T(8,128)}, u32[]{:S(2)}) copy-start(f32[192,96]{1,0:T(8,128)} %param.33) | copy-start | bytes 221188
  1387.5 48.4 %copy-start.32 = (f32[192,96]{1,0:T(8,128)S(1)}, f32[192,96]{1,0:T(8,128)}, u32[]{:S(2)}) copy-start(f32[192,96]{1,0:T(8,128)} %param.39) | copy-start | bytes 221188
  1387.5 48.4 %copy-start.33 = (f32[192,96]{1,0:T(8,128)S(1)}, f32[192,96]{1,0:T(8,128)}, u32[]{:S(2)}) copy-start(f32[192,96]{1,0:T(8,128)} %param.45) | copy-start | bytes 221188
  1387.5 49.2 %copy-start.27 = (f32[512,96]{0,1:T(8,128)S(1)}, f32[512,96]{0,1:T(8,128)}, u32[]{:S(2)}) copy-start(f32[512,96]{0,1:T(8,128)} %param.35) | copy-start | bytes 589828
  1387.5 49.2 %copy-start.28 = (f32[512,96]{0,1:T(8,128)S(1)}, f32[512,96]{0,1:T(8,128)}, u32[]{:S(2)}) copy-start(f32[512,96]{0,1:T(8,128)} %reduce-scatter.14.cloned.1.call-done) | copy-start | bytes 589828
  1387.5 49.2 %copy-start.31 = (f32[512,96]{0,1:T(8,128)S(1)}, f32[512,96]{0,1:T(8,128)}, u32[]{:S(2)}) copy-start(f32[512,96]{0,1:T(8,128)} %param.41) | copy-start | bytes 589828
  1387.5 51.0 %copy-start.19 = (f32[2,96,512]{2,1,0:T(8,128)S(1)}, f32[2,96,512]{2,1,0:T(8,128)}, u32[]{:S(2)}) copy-start(f32[2,96,512]{2,1,0:T(8,128)} %param.34) | copy-start | bytes 1179652
  1387.5 51.0 %copy-start.20 = (f32[2,96,512]{2,1,0:T(8,128)S(1)}, f32[2,96,512]{2,1,0:T(8,128)}, u32[]{:S(2)}) copy-start(f32[2,96,512]{2,1,0:T(8,128)} %reduce-scatter.12.cloned.1.call-done) | copy-start | bytes 1179652
  1427.4 7.1 copy-start.46
  (38 other events, 130.8 us)
Sparse Core Ops, SparseCore 0:
  10.8 64.3 all-gather.4
  277.4 119.5 all-gather.6
  425.1 94.0 all-reduce.8
  522.0 55.8 all-reduce.6
  940.2 94.0 all-reduce.10
  1037.6 65.0 reduce-scatter.13
  1106.3 61.3 reduce-scatter.17
  1171.6 60.4 reduce-scatter.19
  1236.1 65.6 reduce-scatter.15
  1305.7 73.1 reduce-scatter.11
